TPU v7x, 32 devices: a whole 2x2x4 slice. The times are simulated.
32 devices in a mesh: shard: 4 (over z), ctx: 2 (over x), tp: 4 (over y, core).
Axes of the slice: x: 2, y: 2, z: 4, core: 2. Of those that a mesh axis runs over, the one named last changes fastest.
Arguments:
- tokens: bfloat16 [4, 1024, 768], P('shard', 'ctx'), may hold values from -6 to 6
- segment_ids: int32 [4, 1024], P('shard', 'ctx'), may hold values from 0 to 15, never falling along the last dimension, each value on 1 to 512 neighbouring positions
- valid_mask: int32 [4, 1024], P('shard', 'ctx'), may hold values from 0 to 1, as said below
- qkv_weight: bfloat16 [3, 768, 768], P(None, ('shard', 'ctx'), 'tp'), may hold values from -0.21875 to 0.21875
- qv_bias: float32 [2, 768], P(None, 'tp'), may hold values from -0.4375 to 0.4375
- out_weight: bfloat16 [768, 768], P('tp', ('shard', 'ctx')), may hold values from -2.5 to 2.5
- out_bias: float32 [768], replicated, may hold values from -1.5 to 1.5
- norm1_gain: float32 [768], replicated, may hold values from 0.5 to 1.5
- norm1_shift: float32 [768], replicated, may hold values from -1.5 to 1.5
- in_weight: bfloat16 [768, 3072], P(('shard', 'ctx'), 'tp'), may hold values from -0.21875 to 0.21875
- in_bias: float32 [3072], P('tp'), may hold values from -4 to 4
- down_weight: bfloat16 [3072, 768], P('tp', ('shard', 'ctx')), may hold values from -0.109375 to 0.109375
- down_bias: float32 [768], replicated, may hold values from -1.5 to 1.5
- norm2_gain: float32 [768], replicated, may hold values from 0.5 to 1.5
- norm2_shift: float32 [768], replicated, may hold values from -1.5 to 1.5
- out_cotangent: float32 [4, 1024, 768], P('shard', 'ctx'), may hold values from -6 to 6
Outputs:
- layer_out: bfloat16 [4, 1024, 768], P('shard', 'ctx')
- tokens_grad: float32 [4, 1024, 768], P('shard', 'ctx')
- qkv_weight_grad: float32 [3, 768, 768], P(None, ('shard', 'ctx'), 'tp')
- qv_bias_grad: float32 [2, 768], P(None, 'tp')
- out_weight_grad: float32 [768, 768], P('tp', ('shard', 'ctx'))
- out_bias_grad: float32 [768], replicated
- norm1_gain_grad: float32 [768], replicated
- norm1_shift_grad: float32 [768], replicated
- in_weight_grad: float32 [768, 3072], P(('shard', 'ctx'), 'tp')
- in_bias_grad: float32 [3072], P('tp')
- down_weight_grad: float32 [3072, 768], P('tp', ('shard', 'ctx'))
- down_bias_grad: float32 [768], replicated
- norm2_gain_grad: float32 [768], replicated
- norm2_shift_grad: float32 [768], replicated
- stream_rms: float32 [3], replicated
Inputs may be any that keep to these rules, and one draw needn't show every extreme that they name: `segment_ids`: in each sequence the document numbers never fall; each of the 16 documents holds 1 to 512 tokens, and one holds exactly 512. In each sequence the tokens with valid_mask 1 are a leading run of 512 to 1024 positions.
All inputs are finite; a program needn't handle non-finite values.
Results may differ from a plain program's by a relative error of at most 0.012.
Values may be sent and summed in bfloat16 or wider, within the bound.
A program may use at most 128 MiB of HBM per device.

v0:
```python
import jax
import jax.numpy as jnp
from jax import lax
from jax.sharding import PartitionSpec as P

HEAD_DIM = 64
norm_eps = 1e-12
masked_score = -1e30


def layer_norm(rows, gain, shift):
    mean = jnp.mean(rows, axis=-1, keepdims=True)
    centred = rows - mean
    spread = jnp.mean(centred * centred, axis=-1, keepdims=True)
    return centred * lax.rsqrt(spread + norm_eps) * gain + shift


def gelu_tanh(value):
    return jax.nn.gelu(value, approximate=True)


def allowed_pairs(query_seg, query_pos, key_seg, key_valid, key_pos):
    same = query_seg[:, None] == key_seg[None, :]
    usable = (key_valid[None, :] == 1) | (query_pos[:, None] == key_pos[None, :])
    return same & usable


def scaled_scores(left, right):
    return jnp.einsum("ae,be->ab", left, right, preferred_element_type=jnp.float32) * 0.125


def softmax_parts(scores, mask):
    masked = jnp.where(mask, scores, masked_score)
    top = jnp.max(masked, axis=1)
    weights = jnp.where(mask, jnp.exp(masked - top[:, None]), 0.0)
    return (top, jnp.sum(weights, axis=1), weights)


def rebuilt_probs(scores, mask, top, total):
    masked = jnp.where(mask, scores, masked_score)
    weights = jnp.where(mask, jnp.exp(masked - top[:, None]), 0.0)
    return weights / total[:, None]


def body(
    tokens,
    segment_ids,
    valid_mask,
    qkv_weight,
    qv_bias,
    out_weight,
    out_bias,
    norm1_gain,
    norm1_shift,
    in_weight,
    in_bias,
    down_weight,
    down_bias,
    norm2_gain,
    norm2_shift,
    out_cotangent,
):
    seqs_here, piece, width = tokens.shape
    rows = seqs_here * piece
    cols = qkv_weight.shape[2]
    heads_here = cols // HEAD_DIM
    w_qkv, w_out, w_in, w_down = (
        lax.all_gather(qkv_weight, ("shard", "ctx"), axis=1, tiled=True),
        lax.all_gather(out_weight, ("shard", "ctx"), axis=1, tiled=True),
        lax.all_gather(in_weight, ("shard", "ctx"), axis=0, tiled=True),
        lax.all_gather(down_weight, ("shard", "ctx"), axis=1, tiled=True),
    )
    flat = tokens.reshape(rows, width)
    projected = jnp.einsum("nd,jdc->jnc", flat, w_qkv, preferred_element_type=jnp.float32)
    queries = (projected[0] + qv_bias[0]).astype(jnp.bfloat16).reshape(seqs_here, piece, cols)
    keys = projected[1].astype(jnp.bfloat16).reshape(seqs_here, piece, cols)
    values = (projected[2] + qv_bias[1]).astype(jnp.bfloat16).reshape(seqs_here, piece, cols)
    marks = lax.all_gather(jnp.stack([segment_ids, valid_mask]), "ctx", axis=2, tiled=True)
    kv_all = lax.all_gather(jnp.stack([keys, values]), "ctx", axis=2, tiled=True)
    seq_len = kv_all.shape[2]
    own_pos = lax.axis_index("ctx") * piece + lax.iota(jnp.int32, piece)
    all_pos = lax.iota(jnp.int32, seq_len)
    seq = 0
    mask = allowed_pairs(segment_ids[seq], own_pos, marks[0, seq], marks[1, seq], all_pos)
    masks = [mask]
    head_tops = []
    head_totals = []
    head_out = []
    for head in range(heads_here):
        span = slice(head * HEAD_DIM, (head + 1) * HEAD_DIM)
        scores = scaled_scores(queries[seq, :, span], kv_all[0, seq, :, span])
        top, total, weights = softmax_parts(scores, mask)
        probs = (weights / total[:, None]).astype(jnp.bfloat16)
        head_out.append(jnp.dot(probs, kv_all[1, seq, :, span], preferred_element_type=jnp.float32))
        head_tops.append(top)
        head_totals.append(total)
    context_parts = [jnp.concatenate(head_out, axis=1)]
    seq_tops = [jnp.stack(head_tops)]
    seq_totals = [jnp.stack(head_totals)]
    context = jnp.stack(context_parts).reshape(rows, cols).astype(jnp.bfloat16)
    top_all = jnp.stack(seq_tops)
    total_all = jnp.stack(seq_totals)
    attn = lax.psum(jnp.dot(context, w_out, preferred_element_type=jnp.float32), "tp") + out_bias
    hidden, norm1_back = jax.vjp(
        layer_norm, flat.astype(jnp.float32) + attn, norm1_gain, norm1_shift
    )
    hidden_low = hidden.astype(jnp.bfloat16)
    pre = jnp.dot(hidden_low, w_in, preferred_element_type=jnp.float32) + in_bias
    act, gelu_back = jax.vjp(gelu_tanh, pre)
    act_low = act.astype(jnp.bfloat16)
    ffn = lax.psum(jnp.dot(act_low, w_down, preferred_element_type=jnp.float32), "tp") + down_bias
    out_rows, norm2_back = jax.vjp(layer_norm, hidden + ffn, norm2_gain, norm2_shift)
    layer_out = out_rows.astype(jnp.bfloat16).reshape(seqs_here, piece, width)
    w_qkv, w_out, w_in, w_down = (
        lax.all_gather(qkv_weight, ("shard", "ctx"), axis=1, tiled=True),
        lax.all_gather(out_weight, ("shard", "ctx"), axis=1, tiled=True),
        lax.all_gather(in_weight, ("shard", "ctx"), axis=0, tiled=True),
        lax.all_gather(down_weight, ("shard", "ctx"), axis=1, tiled=True),
    )
    d_resid2, d_gain2, d_shift2 = norm2_back(out_cotangent.reshape(rows, width))
    d_ffn = d_resid2.astype(jnp.bfloat16)
    d_down_bias = jnp.sum(d_ffn.astype(jnp.float32), axis=0)
    g_down = jnp.einsum("nf,nd->fd", act_low, d_ffn, preferred_element_type=jnp.float32)
    d_act = jnp.einsum("nd,fd->nf", d_ffn, w_down, preferred_element_type=jnp.float32)
    d_pre = gelu_back(d_act)[0].astype(jnp.bfloat16)
    d_in_bias = jnp.sum(d_pre.astype(jnp.float32), axis=0)
    g_in = jnp.einsum("nd,nf->df", hidden_low, d_pre, preferred_element_type=jnp.float32)
    d_hidden = d_resid2 + lax.psum(
        jnp.einsum("nf,df->nd", d_pre, w_in, preferred_element_type=jnp.float32), "tp"
    )
    d_resid1, d_gain1, d_shift1 = norm1_back(d_hidden)
    d_attn = d_resid1.astype(jnp.bfloat16)
    d_out_bias = jnp.sum(d_attn.astype(jnp.float32), axis=0)
    g_out = jnp.einsum("nc,nd->cd", context, d_attn, preferred_element_type=jnp.float32)
    d_context = (
        jnp.einsum("nd,cd->nc", d_attn, w_out, preferred_element_type=jnp.float32)
        .astype(jnp.bfloat16)
        .reshape(seqs_here, piece, cols)
    )
    delta_parts = []
    seq = 0
    dq_heads = []
    dk_heads = []
    dv_heads = []
    delta_heads = []
    for head in range(heads_here):
        span = slice(head * HEAD_DIM, (head + 1) * HEAD_DIM)
        q_head = queries[seq, :, span]
        k_every = kv_all[0, seq, :, span]
        d_head = d_context[seq, :, span]
        probs = rebuilt_probs(
            scaled_scores(q_head, k_every), masks[seq], top_all[seq, head], total_all[seq, head]
        )
        d_probs = jnp.einsum(
            "qe,ke->qk", d_head, kv_all[1, seq, :, span], preferred_element_type=jnp.float32
        )
        delta = jnp.sum(probs * d_probs, axis=1)
        d_scores = (probs * (d_probs - delta[:, None])).astype(jnp.bfloat16)
        dq_heads.append(jnp.dot(d_scores, k_every, preferred_element_type=jnp.float32) * 0.125)
        delta_heads.append(delta)
        dk_heads.append(
            jnp.einsum("qk,qe->ke", d_scores, q_head, preferred_element_type=jnp.float32) * 0.125
        )
        dv_heads.append(
            jnp.einsum(
                "qk,qe->ke", probs.astype(jnp.bfloat16), d_head, preferred_element_type=jnp.float32
            )
        )
    query_parts = [jnp.concatenate(dq_heads, axis=1)]
    delta_parts.append(jnp.stack(delta_heads))
    key_parts = [jnp.concatenate(dk_heads, axis=1)]
    value_parts = [jnp.concatenate(dv_heads, axis=1)]
    d_queries = jnp.stack(query_parts).reshape(rows, cols).astype(jnp.bfloat16)
    key_sums, value_sums = (
        lax.psum_scatter(jnp.stack(key_parts), "ctx", scatter_dimension=1, tiled=True),
        lax.psum_scatter(jnp.stack(value_parts), "ctx", scatter_dimension=1, tiled=True),
    )
    d_keys = key_sums.reshape(rows, cols).astype(jnp.bfloat16)
    d_values = value_sums.reshape(rows, cols).astype(jnp.bfloat16)
    d_proj = jnp.stack([d_queries, d_keys, d_values])
    g_qkv = jnp.einsum("nd,jnc->jdc", flat, d_proj, preferred_element_type=jnp.float32)
    d_qv_bias = jnp.stack(
        [
            jnp.sum(d_queries.astype(jnp.float32), axis=0),
            jnp.sum(d_values.astype(jnp.float32), axis=0),
        ]
    )
    d_flat = d_resid1 + lax.psum(
        jnp.einsum("jnc,jdc->nd", d_proj, w_qkv, preferred_element_type=jnp.float32), "tp"
    )
    tokens_grad = d_flat.reshape(seqs_here, piece, width)
    g_qkv_own, g_out_own, g_in_own, g_down_own = (
        lax.psum_scatter(g_qkv, ("shard", "ctx"), scatter_dimension=1, tiled=True),
        lax.psum_scatter(g_out, ("shard", "ctx"), scatter_dimension=1, tiled=True),
        lax.psum_scatter(g_in, ("shard", "ctx"), scatter_dimension=0, tiled=True),
        lax.psum_scatter(g_down, ("shard", "ctx"), scatter_dimension=1, tiled=True),
    )
    valid_rows = valid_mask.reshape(rows, 1).astype(jnp.float32)
    x_rows = flat.astype(jnp.float32)
    stats = jnp.stack(
        [
            jnp.sum(valid_rows * x_rows * x_rows),
            jnp.sum(valid_rows * attn * attn),
            jnp.sum(valid_rows * ffn * ffn),
            jnp.sum(valid_rows),
        ]
    )
    summed = lax.psum(
        (
            d_qv_bias,
            d_out_bias,
            d_gain1,
            d_shift1,
            d_in_bias,
            d_down_bias,
            d_gain2,
            d_shift2,
            stats,
        ),
        ("shard", "ctx"),
    )
    totals = summed[8]
    stream_rms = jnp.sqrt(totals[:3] / (totals[3] * width))
    return (
        layer_out,
        tokens_grad,
        g_qkv_own,
        summed[0],
        g_out_own,
        summed[1],
        summed[2],
        summed[3],
        g_in_own,
        summed[4],
        g_down_own,
        summed[5],
        summed[6],
        summed[7],
        stream_rms,
    )


def solution(mesh):
    return jax.shard_map(
        body,
        mesh=mesh,
        in_specs=(
            P("shard", "ctx", None),
            P("shard", "ctx"),
            P("shard", "ctx"),
            P(None, ("shard", "ctx"), "tp"),
            P(None, "tp"),
            P("tp", ("shard", "ctx")),
            P(),
            P(),
            P(),
            P(("shard", "ctx"), "tp"),
            P("tp"),
            P("tp", ("shard", "ctx")),
            P(),
            P(),
            P(),
            P("shard", "ctx", None),
        ),
        out_specs=(
            P("shard", "ctx", None),
            P("shard", "ctx", None),
            P(None, ("shard", "ctx"), "tp"),
            P(None, "tp"),
            P("tp", ("shard", "ctx")),
            P(),
            P(),
            P(),
            P(("shard", "ctx"), "tp"),
            P("tp"),
            P("tp", ("shard", "ctx")),
            P(),
            P(),
            P(),
            P(),
        ),
        check_vma=False,
    )
```

profile of v0, /device:TPU:0, one launch (start us, length us, event | category | flops | bytes accessed | tf_op | source)
XLA Modules:
  0.0 687.0 jit_solution(15073184442933198201)
XLA Ops:
  8.8 5.2 all_gather.22
  15.9 38.3 %all_gather.23 = bf16[3,768,192]{2,0,1:T(4,128)(2,1)S(1)} all-gather(bf16[3,96,192]{2,0,1:T(4,128)(2,1)S(1)} %copy.34), channel_id=1, replica_groups=mesh['shard'=4,'ctx'=2,'tp'=4] {'shard','ctx'}, dimensions={1}, use_global_device_ids=true | all-gather | bytes 995328 | tf_op jit(solution)/shard_map/all_gather | solution.py:68
  55.7 8.5 %all_gather.24 = bf16[2,1,1024,192]{2,3,1,0:T(8,128)(2,1)S(1)} all-gather(bf16[2,1,512,192]{2,3,1,0:T(8,128)(2,1)S(1)} %pad_maximum_fusion.1), channel_id=1, replica_groups=mesh['shard'=4,'ctx'=2,'tp'=4] {'ctx'}, dimensions={2}, use_global_device_ids=true | all-gather | bytes 1179648 | tf_op jit(solution)/shard_map/all_gather | solution.py:79
  70.9 31.2 %all_gather.25 = bf16[192,768]{0,1:T(8,128)(2,1)S(1)} all-gather(bf16[192,96]{0,1:T(8,128)(2,1)S(1)} %copy.36), channel_id=1, replica_groups=mesh['shard'=4,'ctx'=2,'tp'=4] {'shard','ctx'}, dimensions={1}, use_global_device_ids=true | all-gather | bytes 331776 | tf_op jit(solution)/shard_map/all_gather | solution.py:69
  102.1 4.2 fusion.13
  113.6 41.2 %all-reduce.6.cloned.1.call-done = f32[512,768]{1,0:T(8,128)} async-done(((f32[512,768]{1,0:T(8,128)}), f32[512,768]{1,0:T(8,128)}) %all-reduce.6.cloned.1.call-update) | async-done | bytes 1572880 | tf_op jit(solution)/shard_map/psum | solution.py:103
  160.5 37.3 %all-gather.5.cloned.1.call-done = bf16[768,768]{0,1:T(8,128)(2,1)} async-done(((bf16[768,96]{0,1:T(8,128)(2,1)}), bf16[768,768]{0,1:T(8,128)(2,1)}) %all-gather.5.cloned.1.call-update) | async-done | bytes 1179664 | tf_op jit(solution)/shard_map/all_gather | solution.py:71
  197.8 4.0 fusion.48
  203.5 39.9 %all-reduce.8.cloned.1.call-done = f32[512,768]{1,0:T(8,128)} async-done(((f32[512,768]{1,0:T(8,128)}), f32[512,768]{1,0:T(8,128)}) %all-reduce.8.cloned.1.call-update) | async-done | bytes 1572880 | tf_op jit(solution)/shard_map/psum | solution.py:111
  243.3 3.6 fusion.9
  260.9 40.4 %all-reduce.10.cloned.1.call-done = f32[512,768]{1,0:T(8,128)} async-done(((f32[512,768]{1,0:T(8,128)}), f32[512,768]{1,0:T(8,128)}) %all-reduce.10.cloned.1.call-update) | async-done | bytes 1572880 | tf_op jit(solution)/shard_map/psum | solution.py:128
  330.6 4.6 reduce-scatter.11.cloned.1.call-done
  336.3 18.6 %reduce-scatter.13.cloned.1.call-done = f32[1,512,192]{1,2,0:T(8,128)} async-done(((f32[1,1024,192]{1,2,0:T(8,128)}), f32[1,512,192]{1,2,0:T(8,128)}) %reduce-scatter.13.cloned.1.call-update) | async-done | bytes 393232 | tf_op jit(solution)/shard_map/reduce_scatter | solution.py:176
  357.3 3.4 convolution_bitcast_fusion.1
  363.9 4.2 copy.39
  368.1 4.7 reshape.271
  373.5 3.5 fusion.49
  378.1 3.8 fusion.47
  386.0 34.5 %reduce-scatter.21.cloned.1.call-done = f32[96,192]{1,0:T(8,128)} async-done(((f32[768,192]{1,0:T(8,128)}), f32[96,192]{1,0:T(8,128)}) %reduce-scatter.21.cloned.1.call-update) | async-done | bytes 73744
  422.2 35.7 %all-reduce = (f32[2,192]{1,0:T(2,128)}, f32[768]{0:T(1024)}, f32[768]{0:T(1024)}, f32[768]{0:T(1024)}, f32[768]{0:T(1024)}, /*index=5*/f32[768]{0:T(1024)}, f32[768]{0:T(1024)}, f32[768]{0:T(1024)}, f32[4]{0:T(128)S(1)}) all-reduce(f32[2,192]{1,0:T(2,128)S(1)} %pad_maximum_fusion.5, ...), channel_id=1, replica_groups=mesh['shard'=4,'ctx'=2,'tp'=4] {'shard','ctx'}, use_global_device_ids=true, to_apply=%region_26.27 | all-reduce | flops 5764 | bytes 46112 | tf_op jit(solution)/shard_map/psum | solution.py:208
  459.7 5.2 all-reduce.12.cloned.1.call-done
  467.7 67.9 %reduce-scatter.19.cloned.1.call-done = f32[96,576]{1,0:T(8,128)} async-done(((f32[768,576]{1,0:T(8,128)}), f32[96,576]{1,0:T(8,128)}) %reduce-scatter.19.cloned.1.call-update) | async-done | bytes 221200
  537.5 70.1 %reduce-scatter.15.cloned.1.call-done = f32[96,768]{1,0:T(8,128)} async-done(((f32[768,768]{1,0:T(8,128)}), f32[96,768]{1,0:T(8,128)}) %reduce-scatter.15.cloned.1.call-update) | async-done | bytes 294928 | tf_op jit(solution)/shard_map/reduce_scatter | solution.py:195
  607.6 72.0 %reduce-scatter.17.cloned.1.call-done = f32[768,96]{0,1:T(8,128)} async-done(((f32[768,768]{0,1:T(8,128)}), f32[768,96]{0,1:T(8,128)}) %reduce-scatter.17.cloned.1.call-update) | async-done | bytes 294928 | tf_op jit(solution)/shard_map/reduce_scatter | solution.py:196
  (259 shorter events, 87.6 us)
Async XLA Ops:
  8.0 46.3 %copy-start.15 = (bf16[1,512,768]{2,1,0:T(8,128)(2,1)S(1)}, bf16[1,512,768]{2,1,0:T(8,128)(2,1)}, u32[]{:S(2)}) copy-start(bf16[1,512,768]{2,1,0:T(8,128)(2,1)} %param.16) | copy-start | bytes 2359300
  8.0 146.7 %all-reduce.6.cloned.1.call-start = ((), (), s32[]{:S(2)}) async-start(), calls=%async_computation.6 | async-start | bytes 3145728 | tf_op jit(solution)/shard_map/psum | solution.py:103
  14.1 95.0 %copy-start.63 = (pred[1024]{0:T(1024)(128)(4,1)}, pred[1024]{0:T(1024)(128)(4,1)S(1)}, u32[]{:S(2)}) copy-start(pred[1024]{0:T(1024)(128)(4,1)S(1)} %compare_reduce_fusion) | copy-start | bytes 3076
  14.1 95.0 %copy-start.45 = (s32[1,1,1024]{2,1,0:T(1,128)}, s32[1,1,1024]{2,1,0:T(1,128)S(1)}, u32[]{:S(2)}) copy-start(s32[1,1,1024]{2,1,0:T(1,128)S(1)} %slice.118) | copy-start | bytes 12292
  14.1 95.0 %copy-start.57 = (s32[512]{0:T(512)}, s32[512]{0:T(512)S(1)}, u32[]{:S(2)}) copy-start(s32[512]{0:T(512)S(1)} %iota_add_fusion) | copy-start | bytes 6148
  64.2 45.0 %copy-start.16 = (bf16[2,1,1024,192]{2,3,1,0:T(8,128)(2,1)}, bf16[2,1,1024,192]{2,3,1,0:T(8,128)(2,1)S(1)}, u32[]{:S(2)}) copy-start(bf16[2,1,1024,192]{2,3,1,0:T(8,128)(2,1)S(1)} %all_gather.24) | copy-start | bytes 2359300
  66.4 41.2 %copy-start.51 = (f32[512]{0:T(512)}, f32[512]{0:T(512)S(1)}, u32[]{:S(2)}) copy-start(f32[512]{0:T(512)S(1)} %get-tuple-element.107) | copy-start | bytes 6148
  68.6 40.6 %copy-start.52 = (f32[512]{0:T(512)}, f32[512]{0:T(512)S(1)}, u32[]{:S(2)}) copy-start(f32[512]{0:T(512)S(1)} %get-tuple-element.105) | copy-start | bytes 6148
  110.7 44.0 %copy-start.47 = (f32[768]{0:T(1024)S(1)}, f32[768]{0:T(1024)}, u32[]{:S(2)}) copy-start(f32[768]{0:T(1024)} %param.22) | copy-start | bytes 9220
  112.3 44.5 %all-gather.3.cloned.1.call-start = ((), (), s32[]{:S(2)}) async-start(), calls=%async_computation.7 | async-start | bytes 1327104 | tf_op jit(solution)/shard_map/all_gather | solution.py:70
  112.9 84.9 %all-gather.5.cloned.1.call-start = ((), (), s32[]{:S(2)}) async-start(), calls=%async_computation.8 | async-start | bytes 1327104 | tf_op jit(solution)/shard_map/all_gather | solution.py:71
  113.5 129.8 %all-reduce.8.cloned.1.call-start = ((), (), s32[]{:S(2)}) async-start(), calls=%async_computation.9 | async-start | bytes 3145728 | tf_op jit(solution)/shard_map/psum | solution.py:111
  201.8 41.5 %copy-start.14 = (f32[512,768]{1,0:T(8,128)S(1)}, f32[512,768]{1,0:T(8,128)}, u32[]{:S(2)}) copy-start(f32[512,768]{1,0:T(8,128)} %all-reduce.6.cloned.1.call-done) | copy-start | bytes 4718596
  201.8 99.5 %all-reduce.10.cloned.1.call-start = ((), (), s32[]{:S(2)}) async-start(), calls=%async_computation.10 | async-start | bytes 3145728 | tf_op jit(solution)/shard_map/psum | solution.py:128
  258.3 77.0 %reduce-scatter.11.cloned.1.call-start = ((), (), s32[]{:S(2)}) async-start(), calls=%async_computation.11 | async-start | bytes 1179648 | tf_op jit(solution)/shard_map/reduce_scatter | solution.py:175
  317.6 37.3 %reduce-scatter.13.cloned.1.call-start = ((), (), s32[]{:S(2)}) async-start(), calls=%async_computation.12 | async-start | bytes 1179648 | tf_op jit(solution)/shard_map/reduce_scatter | solution.py:176
  323.0 97.5 %reduce-scatter.21.cloned.1.call-start = ((), (), s32[]{:S(2)}) async-start(), calls=%async_computation.17 | async-start | bytes 884736
  325.8 139.2 %all-reduce.12.cloned.1.call-start = ((), (), s32[]{:S(2)}) async-start(), calls=%async_computation.13 | async-start | bytes 3145728 | tf_op jit(solution)/shard_map/psum | solution.py:188
  360.7 174.9 %reduce-scatter.19.cloned.1.call-start = ((), (), s32[]{:S(2)}) async-start(), calls=%async_computation.16 | async-start | bytes 2211840
  372.8 234.8 %reduce-scatter.15.cloned.1.call-start = ((), (), s32[]{:S(2)}) async-start(), calls=%async_computation.14 | async-start | bytes 2654208 | tf_op jit(solution)/shard_map/reduce_scatter | solution.py:195
  377.0 302.6 %reduce-scatter.17.cloned.1.call-start = ((), (), s32[]{:S(2)}) async-start(), calls=%async_computation.15 | async-start | bytes 2654208 | tf_op jit(solution)/shard_map/reduce_scatter | solution.py:196
  382.0 40.2 %copy-start.65 = (f32[192]{0:T(256)S(1)}, f32[192]{0:T(256)}, u32[]{:S(2)}) copy-start(f32[192]{0:T(256)} %get-tuple-element.71) | copy-start | bytes 2308
  382.0 40.2 %copy-start.42 = (f32[768]{0:T(1024)S(1)}, f32[768]{0:T(1024)}, u32[]{:S(2)}) copy-start(f32[768]{0:T(1024)} %get-tuple-element.45) | copy-start | bytes 9220
  382.1 82.9 %copy-start.2 = (f32[512,768]{1,0:T(8,128)S(1)}, f32[512,768]{1,0:T(8,128)}, u32[]{:S(2)}) copy-start(f32[512,768]{1,0:T(8,128)} %copy-done.1) | copy-start | bytes 4718596
  (67 other events, 366.2 us)
Sparse Core Ops, SparseCore 0:
  112.5 42.2 all-reduce.5
  202.0 41.3 all-reduce.7
  258.4 42.8 all-reduce.9
  317.7 17.4 reduce-scatter.10
  337.4 17.4 reduce-scatter.12
  358.1 62.4 reduce-scatter.20
  423.0 41.8 all-reduce.11
  468.8 66.7 reduce-scatter.18
  539.7 67.8 reduce-scatter.14
  611.5 68.0 reduce-scatter.16
Sparse Core Ops, SparseCore 1:
  115.0 40.7 all-gather.2
  157.8 40.0 all-gather.4
where the time goes:
time: 688 us; the launch traced here: 687 us
  waiting for transfers between devices  433 us (63%)
  blocking collectives  119 us (17%)
  matrix products  53 us (8%)
  other arithmetic  34.3 us (5%)
  local copies, waits for them, and re-layouts  29.7 us (4%)
  between operations  17.2 us (2%)
    unnamed x14, waiting for transfers between devices  104 us
    reduce_scatter x1, waiting for transfers between devices, body(): lax.psum_scatter(g_down, ('shard', 'ctx'), scatter_dimension=1, tiled=True)  72 us
    reduce_scatter x1, waiting for transfers between devices, body(): lax.psum_scatter(g_in, ('shard', 'ctx'), scatter_dimension=0, tiled=True)  70.1 us
    psum x1, waiting for transfers between devices, body(): lax.psum(jnp.dot(context, w_out, preferred_element_type=jnp.float32), 'tp')  41.2 us
    psum x1, waiting for transfers between devices, body(): lax.psum(jnp.einsum('nf,df->nd', d_pre, w_in, preferred_element_type=jnp....  40.4 us
    psum x1, waiting for transfers between devices, body(): lax.psum(jnp.dot(act_low, w_down, preferred_element_type=jnp.float32), 'tp')  39.9 us
    all_gather x1, blocking collectives, body(): lax.all_gather(qkv_weight, ('shard', 'ctx'), axis=1, tiled=True)  38.3 us
    all_gather x1, waiting for transfers between devices, body(): lax.all_gather(down_weight, ('shard', 'ctx'), axis=1, tiled=True)  37.3 us
  transfers between devices with their start and end apart: 12, of which 11 were waited for; matrix products, arithmetic and copies ran while one was open for 8% of the time, Pallas kernels for 0%

commit v1 on v0

--- a/solution.py
+++ b/solution.py
@@ -6,6 +6,18 @@
 HEAD_DIM = 64
 norm_eps = 1e-12
 masked_score = -1e30
+
+
+def doubled_up(x, axis, dim):
+    ways, here = (lax.axis_size(axis), lax.axis_index(axis))
+    grown, reach = (x, 1)
+    while reach < ways:
+        theirs = lax.ppermute(grown, axis, [(d, d ^ reach) for d in range(ways)])
+        mine_first = jnp.concatenate([grown, theirs], axis=dim)
+        theirs_first = jnp.concatenate([theirs, grown], axis=dim)
+        grown = jnp.where(here & reach == 0, mine_first, theirs_first)
+        reach = 2 * reach
+    return grown
 
 
 def layer_norm(rows, gain, shift):
@@ -66,7 +78,7 @@
     heads_here = cols // HEAD_DIM
     w_qkv, w_out, w_in, w_down = (
         lax.all_gather(qkv_weight, ("shard", "ctx"), axis=1, tiled=True),
-        lax.all_gather(out_weight, ("shard", "ctx"), axis=1, tiled=True),
+        doubled_up(out_weight, ("shard", "ctx"), 1),
         lax.all_gather(in_weight, ("shard", "ctx"), axis=0, tiled=True),
         lax.all_gather(down_weight, ("shard", "ctx"), axis=1, tiled=True),
     )

time: 688 us -> 663 us (0.964)
  waiting for transfers between devices: 433 us -> 410 us
    psum x1, waiting for transfers between devices: 40.4 us -> 10.1 us  [body(): lax.psum(jnp.einsum('nf,df->nd', d_pre, w_in, preferred_element_type=jnp....]
    unnamed x165 -> x159, local copies, waits for them, and re-layouts: 27.1 us -> 27.8 us
  transfers between devices with their start and end apart: 12 -> 15, of which waited for: 11 -> 13; matrix products, arithmetic and copies ran while one was open for 8% -> 10% of each run, Pallas kernels for 0% -> 0%
where the time goes in v1:
time: 663 us; the launch traced here: 662 us
  waiting for transfers between devices  410 us (62%)
  blocking collectives  117 us (18%)
  matrix products  50.8 us (8%)
  local copies, waits for them, and re-layouts  30.4 us (5%)
  other arithmetic  29.8 us (4%)
  between operations  17.2 us (3%)
    unnamed x14, waiting for transfers between devices  104 us
    reduce_scatter x1, waiting for transfers between devices, body(): lax.psum_scatter(g_down, ('shard', 'ctx'), scatter_dimension=1, tiled=True)  72 us
    reduce_scatter x1, waiting for transfers between devices, body(): lax.psum_scatter(g_in, ('shard', 'ctx'), scatter_dimension=0, tiled=True)  70.7 us
    psum x1, waiting for transfers between devices, body(): lax.psum(jnp.dot(context, w_out, preferred_element_type=jnp.float32), 'tp')  41.3 us
    psum x1, waiting for transfers between devices, body(): lax.psum(jnp.dot(act_low, w_down, preferred_element_type=jnp.float32), 'tp')  40.1 us
    all_gather x1, waiting for transfers between devices, body(): lax.all_gather(down_weight, ('shard', 'ctx'), axis=1, tiled=True)  38.5 us
    all_gather x1, blocking collectives, body(): lax.all_gather(qkv_weight, ('shard', 'ctx'), axis=1, tiled=True)  37.1 us
    psum x1, blocking collectives, body(): lax.psum((d_qv_bias, d_out_bias, d_gain1, d_shift1, d_in_bias, d_down_bia...  35.8 us
  transfers between devices with their start and end apart: 15, of which 13 were waited for; matrix products, arithmetic and copies ran while one was open for 10% of the time, Pallas kernels for 0%

profile of v1, /device:TPU:0, one launch (start us, length us, event | category | flops | bytes accessed | tf_op | source)
XLA Modules:
  0.0 661.8 jit_solution(7252218407377217774)
XLA Ops:
  11.8 4.3 all_gather.21
  18.0 37.1 %all_gather.22 = bf16[3,768,192]{2,0,1:T(4,128)(2,1)S(1)} all-gather(bf16[3,96,192]{2,0,1:T(4,128)(2,1)S(1)} %copy.34), channel_id=1, replica_groups=mesh['shard'=4,'ctx'=2,'tp'=4] {'shard','ctx'}, dimensions={1}, use_global_device_ids=true | all-gather | bytes 995328 | tf_op jit(solution)/shard_map/all_gather | solution.py:80
  56.6 8.5 %all_gather.23 = bf16[2,1,1024,192]{2,3,1,0:T(8,128)(2,1)S(1)} all-gather(bf16[2,1,512,192]{2,3,1,0:T(8,128)(2,1)S(1)} %pad_maximum_fusion.1), channel_id=1, replica_groups=mesh['shard'=4,'ctx'=2,'tp'=4] {'ctx'}, dimensions={2}, use_global_device_ids=true | all-gather | bytes 1179648 | tf_op jit(solution)/shard_map/all_gather | solution.py:91
  81.0 3.4 collective-permute-done.2
  87.4 41.3 %all-reduce.6.cloned.1.call-done = f32[512,768]{1,0:T(8,128)} async-done(((f32[512,768]{1,0:T(8,128)}), f32[512,768]{1,0:T(8,128)}) %all-reduce.6.cloned.1.call-update) | async-done | bytes 1572880 | tf_op jit(solution)/shard_map/psum | solution.py:115
  133.4 38.5 %all-gather.5.cloned.1.call-done = bf16[768,768]{0,1:T(8,128)(2,1)} async-done(((bf16[768,96]{0,1:T(8,128)(2,1)}), bf16[768,768]{0,1:T(8,128)(2,1)}) %all-gather.5.cloned.1.call-update) | async-done | bytes 1179664 | tf_op jit(solution)/shard_map/all_gather | solution.py:83
  171.8 3.5 fusion.54
  176.7 40.1 %all-reduce.8.cloned.1.call-done = f32[512,768]{1,0:T(8,128)} async-done(((f32[512,768]{1,0:T(8,128)}), f32[512,768]{1,0:T(8,128)}) %all-reduce.8.cloned.1.call-update) | async-done | bytes 1572880 | tf_op jit(solution)/shard_map/psum | solution.py:123
  216.8 3.6 fusion.9
  231.9 31.6 %all_gather.26 = bf16[192,768]{0,1:T(8,128)(2,1)S(1)} all-gather(bf16[192,96]{0,1:T(8,128)(2,1)} %copy.36), channel_id=1, replica_groups=mesh['shard'=4,'ctx'=2,'tp'=4] {'shard','ctx'}, dimensions={1}, use_global_device_ids=true | all-gather | bytes 331776 | tf_op jit(solution)/shard_map/all_gather | solution.py:128
  264.8 10.1 %all-reduce.10.cloned.1.call-done = f32[512,768]{1,0:T(8,128)} async-done(((f32[512,768]{1,0:T(8,128)}), f32[512,768]{1,0:T(8,128)}) %all-reduce.10.cloned.1.call-update) | async-done | bytes 1572880 | tf_op jit(solution)/shard_map/psum | solution.py:140
  304.0 4.9 reduce-scatter.11.cloned.1.call-done
  309.9 18.6 %reduce-scatter.13.cloned.1.call-done = f32[1,512,192]{1,2,0:T(8,128)} async-done(((f32[1,1024,192]{1,2,0:T(8,128)}), f32[1,512,192]{1,2,0:T(8,128)}) %reduce-scatter.13.cloned.1.call-update) | async-done | bytes 393232 | tf_op jit(solution)/shard_map/reduce_scatter | solution.py:188
  330.9 3.4 convolution_bitcast_fusion.1
  337.5 4.3 copy.39
  341.8 4.7 reshape.271
  347.2 3.5 fusion.55
  351.9 3.9 fusion.53
  359.7 34.5 %reduce-scatter.21.cloned.1.call-done = f32[96,192]{1,0:T(8,128)} async-done(((f32[768,192]{1,0:T(8,128)}), f32[96,192]{1,0:T(8,128)}) %reduce-scatter.21.cloned.1.call-update) | async-done | bytes 73744
  395.9 35.8 %all-reduce = (f32[2,192]{1,0:T(2,128)}, f32[768]{0:T(1024)}, f32[768]{0:T(1024)}, f32[768]{0:T(1024)}, f32[768]{0:T(1024)}, /*index=5*/f32[768]{0:T(1024)}, f32[768]{0:T(1024)}, f32[768]{0:T(1024)}, f32[4]{0:T(128)S(1)}) all-reduce(f32[2,192]{1,0:T(2,128)S(1)} %pad_maximum_fusion.5, ...), channel_id=1, replica_groups=mesh['shard'=4,'ctx'=2,'tp'=4] {'shard','ctx'}, use_global_device_ids=true, to_apply=%region_26.27 | all-reduce | flops 5764 | bytes 46112 | tf_op jit(solution)/shard_map/psum | solution.py:220
  433.4 5.7 all-reduce.12.cloned.1.call-done
  441.9 67.9 %reduce-scatter.19.cloned.1.call-done = f32[96,576]{1,0:T(8,128)} async-done(((f32[768,576]{1,0:T(8,128)}), f32[96,576]{1,0:T(8,128)}) %reduce-scatter.19.cloned.1.call-update) | async-done | bytes 221200
  511.7 70.7 %reduce-scatter.15.cloned.1.call-done = f32[96,768]{1,0:T(8,128)} async-done(((f32[768,768]{1,0:T(8,128)}), f32[96,768]{1,0:T(8,128)}) %reduce-scatter.15.cloned.1.call-update) | async-done | bytes 294928 | tf_op jit(solution)/shard_map/reduce_scatter | solution.py:207
  582.4 72.0 %reduce-scatter.17.cloned.1.call-done = f32[768,96]{0,1:T(8,128)} async-done(((f32[768,768]{0,1:T(8,128)}), f32[768,96]{0,1:T(8,128)}) %reduce-scatter.17.cloned.1.call-update) | async-done | bytes 294928 | tf_op jit(solution)/shard_map/reduce_scatter | solution.py:208
  (261 shorter events, 92.7 us)
Async XLA Ops:
  8.0 47.1 %copy-start.15 = (bf16[1,512,768]{2,1,0:T(8,128)(2,1)S(1)}, bf16[1,512,768]{2,1,0:T(8,128)(2,1)}, u32[]{:S(2)}) copy-start(bf16[1,512,768]{2,1,0:T(8,128)(2,1)} %param.16) | copy-start | bytes 2359300
  8.0 120.7 %all-reduce.6.cloned.1.call-start = ((), (), s32[]{:S(2)}) async-start(), calls=%async_computation.6 | async-start | bytes 3145728 | tf_op jit(solution)/shard_map/psum | solution.py:115
  8.1 63.7 %collective-permute-start = (bf16[192,96]{1,0:T(8,128)(2,1)}, bf16[192,96]{1,0:T(8,128)(2,1)S(1)}, u32[]{:S(2)}, u32[]{:S(2)}) collective-permute-start(bf16[192,96]{1,0:T(8,128)(2,1)} %param.21), channel_id=1, source_target_pairs={{0,4},{4,0},{8,12},{12,8},{16,20},{20,16},{24,28},{28,24},{1,5},{5... | collective-permute-start | bytes 110600 | tf_op jit(solution)/shard_map/ppermute | solution.py:15
  16.1 62.1 %copy-start.59 = (pred[1024]{0:T(1024)(128)(4,1)}, pred[1024]{0:T(1024)(128)(4,1)S(1)}, u32[]{:S(2)}) copy-start(pred[1024]{0:T(1024)(128)(4,1)S(1)} %compare_reduce_fusion) | copy-start | bytes 3076
  16.1 62.0 %copy-start.46 = (s32[1,1,1024]{2,1,0:T(1,128)}, s32[1,1,1024]{2,1,0:T(1,128)S(1)}, u32[]{:S(2)}) copy-start(s32[1,1,1024]{2,1,0:T(1,128)S(1)} %slice.118) | copy-start | bytes 12292
  16.2 62.0 %copy-start.52 = (s32[512]{0:T(512)}, s32[512]{0:T(512)S(1)}, u32[]{:S(2)}) copy-start(s32[512]{0:T(512)S(1)} %iota_add_fusion) | copy-start | bytes 6148
  71.9 4.7 collective-permute-start.1
  76.7 7.7 %collective-permute-start.2 = (bf16[192,384]{1,0:T(8,128)(2,1)S(1)}, bf16[192,384]{1,0:T(8,128)(2,1)S(1)}, u32[]{:S(2)}, u32[]{:S(2)}) collective-permute-start(bf16[192,384]{1,0:T(8,128)(2,1)S(1)} %maximum_select_fusion.2), channel_id=1, source_target_pairs={{0,16},{4,20},{8,24},{12,28},{16,0},{20,4},{24,8},{28,12},{1,17},{... | collective-permute-start | bytes 442376 | tf_op jit(solution)/shard_map/ppermute | solution.py:15
  80.9 47.8 %copy-start.48 = (f32[768]{0:T(1024)S(1)}, f32[768]{0:T(1024)}, u32[]{:S(2)}) copy-start(f32[768]{0:T(1024)} %param.22) | copy-start | bytes 9220
  86.0 44.8 %all-gather.3.cloned.1.call-start = ((), (), s32[]{:S(2)}) async-start(), calls=%async_computation.7 | async-start | bytes 1327104 | tf_op jit(solution)/shard_map/all_gather | solution.py:82
  86.6 85.2 %all-gather.5.cloned.1.call-start = ((), (), s32[]{:S(2)}) async-start(), calls=%async_computation.8 | async-start | bytes 1327104 | tf_op jit(solution)/shard_map/all_gather | solution.py:83
  87.2 129.7 %all-reduce.8.cloned.1.call-start = ((), (), s32[]{:S(2)}) async-start(), calls=%async_computation.9 | async-start | bytes 3145728 | tf_op jit(solution)/shard_map/psum | solution.py:123
  175.3 41.5 %copy-start.14 = (f32[512,768]{1,0:T(8,128)S(1)}, f32[512,768]{1,0:T(8,128)}, u32[]{:S(2)}) copy-start(f32[512,768]{1,0:T(8,128)} %all-reduce.6.cloned.1.call-done) | copy-start | bytes 4718596
  175.3 41.5 %copy-start.56 = (f32[768]{0:T(1024)S(1)}, f32[768]{0:T(1024)}, u32[]{:S(2)}) copy-start(f32[768]{0:T(1024)} %param.28) | copy-start | bytes 9220
  175.3 99.5 %all-reduce.10.cloned.1.call-start = ((), (), s32[]{:S(2)}) async-start(), calls=%async_computation.10 | async-start | bytes 3145728 | tf_op jit(solution)/shard_map/psum | solution.py:140
  231.8 77.1 %reduce-scatter.11.cloned.1.call-start = ((), (), s32[]{:S(2)}) async-start(), calls=%async_computation.11 | async-start | bytes 1179648 | tf_op jit(solution)/shard_map/reduce_scatter | solution.py:187
  291.2 37.3 %reduce-scatter.13.cloned.1.call-start = ((), (), s32[]{:S(2)}) async-start(), calls=%async_computation.12 | async-start | bytes 1179648 | tf_op jit(solution)/shard_map/reduce_scatter | solution.py:188
  296.4 97.8 %reduce-scatter.21.cloned.1.call-start = ((), (), s32[]{:S(2)}) async-start(), calls=%async_computation.17 | async-start | bytes 884736
  299.1 140.1 %all-reduce.12.cloned.1.call-start = ((), (), s32[]{:S(2)}) async-start(), calls=%async_computation.13 | async-start | bytes 3145728 | tf_op jit(solution)/shard_map/psum | solution.py:200
  334.3 175.5 %reduce-scatter.19.cloned.1.call-start = ((), (), s32[]{:S(2)}) async-start(), calls=%async_computation.16 | async-start | bytes 2211840
  346.5 235.9 %reduce-scatter.15.cloned.1.call-start = ((), (), s32[]{:S(2)}) async-start(), calls=%async_computation.14 | async-start | bytes 2654208 | tf_op jit(solution)/shard_map/reduce_scatter | solution.py:207
  350.7 303.7 %reduce-scatter.17.cloned.1.call-start = ((), (), s32[]{:S(2)}) async-start(), calls=%async_computation.15 | async-start | bytes 2654208 | tf_op jit(solution)/shard_map/reduce_scatter | solution.py:208
  355.8 40.1 %copy-start.43 = (f32[768]{0:T(1024)S(1)}, f32[768]{0:T(1024)}, u32[]{:S(2)}) copy-start(f32[768]{0:T(1024)} %get-tuple-element.45) | copy-start | bytes 9220
  355.8 83.3 %copy-start.2 = (f32[512,768]{1,0:T(8,128)S(1)}, f32[512,768]{1,0:T(8,128)}, u32[]{:S(2)}) copy-start(f32[512,768]{1,0:T(8,128)} %copy-done.1) | copy-start | bytes 4718596
  (67 other events, 432.5 us)
Sparse Core Ops, SparseCore 0:
  86.1 42.5 all-reduce.5
  175.5 41.3 all-reduce.7
  231.9 42.8 all-reduce.9
  291.3 17.4 reduce-scatter.10
  311.0 17.4 reduce-scatter.12
  331.7 62.4 reduce-scatter.20
  397.2 41.8 all-reduce.11
  443.0 66.7 reduce-scatter.18
  513.9 68.4 reduce-scatter.14
  586.3 68.0 reduce-scatter.16
Sparse Core Ops, SparseCore 1:
  88.7 41.0 all-gather.2
  131.8 40.0 all-gather.4
